TPU v7x, 512 devices: a whole 4x8x8 slice. The times are simulated.
512 devices in a mesh: station: 32 (over y, x), tm: 16 (over z, core).
Axes of the slice: x: 4, y: 8, z: 8, core: 2. Of those that a mesh axis runs over, the one named last changes fastest.
Arguments:
- spectra: bfloat16 [16, 128, 4096], P('tm', 'station'), may hold values from -5 to 5
- valid: int32 [16, 128], P('tm', 'station'), may hold values from 0 to 1, as said below
- pair_blocks: int32 [32, 17], P('station'), may hold values from 0 to 31, as said below
Outputs:
- correlations: float32 [8704, 512], P(('station', 'tm'))
Inputs may be any that keep to these rules, and one draw needn't show every extreme that they name: `pair_blocks`: row d begins with d, its 17 entries are distinct, and every unordered pair of blocks appears in some row. `valid`: each station misses one cyclic run of 1 to 7 hours.
All inputs are finite; a program needn't handle non-finite values.
Results may differ from a plain program's by a relative error of at most 0.0026.
Values may be sent and summed in bfloat16 or wider, within the bound.
A program may use at most 64 MiB of HBM per device.

v0:
```python
import math

import jax
import jax.numpy as jnp
from jax import lax
from jax.sharding import PartitionSpec as P

LAGS = 512


def make_lag_table(half_width, lag_count):
    bins = jnp.arange(half_width, dtype=jnp.int32)
    shifts = jnp.arange(lag_count, dtype=jnp.int32) - lag_count // 2
    phase = (2 * bins[:, None] + 1) * shifts[None, :] % (4 * half_width)
    angle = phase.astype(jnp.float32) * (math.pi / (2.0 * half_width))
    return jnp.concatenate([jnp.cos(angle), -jnp.sin(angle)], axis=0).astype(jnp.bfloat16)


def cross_stack(own_block, partner_block, half_width):
    own_real, own_imag = (own_block[..., :half_width], own_block[..., half_width:])
    part_real, part_imag = (partner_block[..., :half_width], partner_block[..., half_width:])
    cross_real = jnp.einsum(
        "haf,hkbf->kabf", own_real, part_real, preferred_element_type=jnp.float32
    ) + jnp.einsum("haf,hkbf->kabf", own_imag, part_imag, preferred_element_type=jnp.float32)
    cross_imag = jnp.einsum(
        "haf,hkbf->kabf", own_imag, part_real, preferred_element_type=jnp.float32
    ) - jnp.einsum("haf,hkbf->kabf", own_real, part_imag, preferred_element_type=jnp.float32)
    return jnp.concatenate([cross_real, cross_imag], axis=-1).astype(jnp.bfloat16)


def per_device(spectra, valid, pair_blocks):
    local_hours, block_len, spec_width = spectra.shape
    half_width = spec_width // 2
    lag_count = LAGS
    stations_axis = lax.axis_size("station")
    slot_count = pair_blocks.shape[1]
    plan = pair_blocks[0]
    masked = spectra * valid[:, :, None].astype(jnp.bfloat16)
    gathered, gathered_flags = (
        lax.all_gather(masked, "station", axis=1, tiled=True),
        lax.all_gather(valid, "station", axis=1, tiled=True),
    )
    gathered = gathered.reshape(local_hours, stations_axis, block_len, spec_width)
    gathered_flags = gathered_flags.reshape(local_hours, stations_axis, block_len)
    partners = jnp.take(gathered, plan, axis=1)
    partner_flags = jnp.take(gathered_flags, plan, axis=1)
    per_slot = block_len * block_len
    pair_count = slot_count * per_slot
    lag_table = make_lag_table(half_width, lag_count)
    stacked = cross_stack(masked, partners, half_width).reshape(pair_count, spec_width)
    partial_value = jnp.dot(stacked, lag_table, preferred_element_type=jnp.float32)
    local_counts = jnp.einsum(
        "ha,hkb->kab", valid.astype(jnp.float32), partner_flags.astype(jnp.float32)
    ).reshape(pair_count)
    summed, counts = (
        lax.psum_scatter(partial_value, "tm", scatter_dimension=0, tiled=True),
        lax.psum_scatter(local_counts, "tm", scatter_dimension=0, tiled=True),
    )
    lag_scale = 4.0 / math.sqrt(half_width)
    return summed * lag_scale / counts[:, None]


def solution(mesh):
    placed = (P("tm", "station", None), P("tm", "station"), P("station", None))
    return jax.shard_map(
        per_device,
        mesh=mesh,
        in_specs=placed,
        out_specs=P(("station", "tm"), None),
        check_vma=False,
    )
```

profile of v0, /device:TPU:1, one launch (start us, length us, event | category | flops | bytes accessed | tf_op | source)
XLA Modules:
  0.0 195.7 jit_solution(14837320123272706570)
XLA Ops:
  6.5 0.7 convert_bitcast_fusion.2
  7.3 1.5 copy_multiply_fusion
  10.1 1.3 dynamic-slice
  12.1 0.8 bitcast_dynamic-update-slice_fusion
  12.8 17.5 %all-reduce = s32[128]{0:T(128)S(1)} all-reduce(s32[128]{0:T(128)S(1)} %bitcast_dynamic-update-slice_fusion), channel_id=1, replica_groups=mesh['station'=32,'tm'=16] {'station'}, use_global_device_ids=true, to_apply=%add | all-reduce | flops 128 | bytes 1024
  31.2 0.8 slice_convert_fusion.1
  32.0 19.2 %cosine_convert_fusion = (bf16[2048,512]{1,0:T(8,128)(2,1)}, bf16[2048,512]{1,0:T(8,128)(2,1)}) fusion(s32[512]{0:T(512)S(1)} %iota_add_fusion, s32[2048]{0:T(1024)S(1)} %multiply_add_fusion), kind=kLoop, calls=%fused_computation.15 | loop fusion | flops 17825792 | bytes 4204544 | tf_op jit(solution)/shard_map/convert.24
  51.2 44.4 %all-gather.2.cloned.1.call-done = bf16[1,128,4096]{2,0,1:T(2,128)(2,1)} async-done(((bf16[1,4,4096]{2,0,1:T(2,128)(2,1)}), bf16[1,128,4096]{2,0,1:T(2,128)(2,1)}) %all-gather.2.cloned.1.call-update) | async-done | bytes 1048592 | tf_op jit(solution)/shard_map/all_gather | solution.py:40
  95.6 7.7 %reduce = bf16[128,4096]{1,0:T(8,128)(2,1)S(1)} reduce(bf16[1,128,4096]{2,0,1:T(2,128)(2,1)} %all-gather.2.cloned.1.call-done, bf16[]{:T(256)} %constant.71), dimensions={0}, to_apply=%all_gather.6.reduce_sub_computation | reduce | bytes 2097154 | tf_op jit(solution)/shard_map/all_gather | solution.py:40
  103.8 1.0 gather_fusion
  105.2 1.2 fusion.11
  106.4 1.2 concatenate.13
  107.6 1.1 concatenate.14
  108.7 0.9 copy-done
  109.6 3.6 %fusion.4 = f32[272,512]{1,0:T(8,128)S(1)} fusion(bf16[2048,512]{1,0:T(8,128)(2,1)} %get-tuple-element.12, bf16[2048,512]{1,0:T(8,128)(2,1)S(1)} %copy-done, bf16[272,2048]{1,0:T(8,128)(2,1)} %concatenate.14, bf16[272,2048]{1,0:T(8,128)(2,1)} %concatenate.13), kind=kOutput, calls=%fused_computation.10 | convolution fusion | flops 1153695744 | bytes 6979584 | tf_op jit(solution)/shard_map/dot_general | solution.py:51
  113.2 32.3 %fusion = f32[24,512]{1,0:T(8,128)S(1)} fusion(f32[272,512]{1,0:T(8,128)S(1)} %fusion.4), kind=kCustom, calls=%all-reduce-scatter | all-reduce-scatter fusion | flops 196609 | bytes 608256
  145.5 1.5 collective-permute-start.3
  146.9 9.1 %collective-permute-start.2 = (f32[24,512]{1,0:T(8,128)S(1)}, f32[24,512]{1,0:T(8,128)S(1)}, u32[]{:S(2)}, u32[]{:S(2)}) collective-permute-start(f32[24,512]{1,0:T(8,128)S(1)} %fusion), channel_id=1, source_target_pairs={{0,3},{1,4},{2,5},{3,6},{4,7},{5,8},{6,9},{7,10},{8,11},{9,12},{10... | collective-permute-start | bytes 147464
  156.0 1.3 collective-permute-start.1
  157.3 3.1 %collective-permute-start = (f32[24,512]{1,0:T(8,128)S(1)}, f32[24,512]{1,0:T(8,128)S(1)}, u32[]{:S(2)}, u32[]{:S(2)}) collective-permute-start(f32[24,512]{1,0:T(8,128)S(1)} %fusion), channel_id=1, source_target_pairs={{0,1},{1,2},{2,3},{3,4},{4,5},{5,6},{6,7},{7,8},{8,9},{9,10},{10,1... | collective-permute-start | bytes 147464
  160.4 1.4 collective-permute-start.4
  163.8 23.6 %all-reduce.2 = f32[272]{0:T(512)S(1)} all-reduce(f32[272]{0:T(512)S(1)} %reshape.156), channel_id=3, replica_groups=mesh['station'=32,'tm'=16] {'tm'}, use_global_device_ids=true, to_apply=%region_1.2.clone | all-reduce | flops 272 | bytes 2176
  187.5 0.7 concatenate.17
  188.2 0.7 fusion.13
  (30 shorter events, 4.0 us)
Async XLA Ops:
  6.5 89.0 %all-gather.2.cloned.1.call-start = ((), (), s32[]{:S(2)}) async-start(), calls=%async_computation | async-start | bytes 2162688 | tf_op jit(solution)/shard_map/all_gather | solution.py:40
  107.6 2.0 %copy-start = (bf16[2048,512]{1,0:T(8,128)(2,1)S(1)}, bf16[2048,512]{1,0:T(8,128)(2,1)}, u32[]{:S(2)}) copy-start(bf16[2048,512]{1,0:T(8,128)(2,1)} %get-tuple-element.11) | copy-start | bytes 6291460
  109.6 52.4 %copy-start.1 = (u32[512]{0:T(512)S(1)}, u32[512]{0:T(512)}, u32[]{:S(2)}) copy-start(u32[512]{0:T(512)} %constant.65) | copy-start | bytes 6148
  145.5 42.0 %collective-permute-start.3 = (f32[24,512]{1,0:T(8,128)S(1)}, f32[24,512]{1,0:T(8,128)S(1)}, u32[]{:S(2)}, u32[]{:S(2)}) collective-permute-start(f32[24,512]{1,0:T(8,128)S(1)} %fusion), channel_id=1, source_target_pairs={{0,4},{1,5},{2,6},{3,7},{4,8},{5,9},{6,10},{7,11},{8,12},{9,13},{1... | collective-permute-start | bytes 147464
  146.9 40.5 %collective-permute-start.2 = (f32[24,512]{1,0:T(8,128)S(1)}, f32[24,512]{1,0:T(8,128)S(1)}, u32[]{:S(2)}, u32[]{:S(2)}) collective-permute-start(f32[24,512]{1,0:T(8,128)S(1)} %fusion), channel_id=1, source_target_pairs={{0,3},{1,4},{2,5},{3,6},{4,7},{5,8},{6,9},{7,10},{8,11},{9,12},{10... | collective-permute-start | bytes 147464
  156.0 31.5 %collective-permute-start.1 = (f32[24,512]{1,0:T(8,128)S(1)}, f32[24,512]{1,0:T(8,128)S(1)}, u32[]{:S(2)}, u32[]{:S(2)}) collective-permute-start(f32[24,512]{1,0:T(8,128)S(1)} %fusion), channel_id=1, source_target_pairs={{0,2},{1,3},{2,4},{3,5},{4,6},{5,7},{6,8},{7,9},{8,10},{9,11},{10,... | collective-permute-start | bytes 147464
  157.3 30.2 %collective-permute-start = (f32[24,512]{1,0:T(8,128)S(1)}, f32[24,512]{1,0:T(8,128)S(1)}, u32[]{:S(2)}, u32[]{:S(2)}) collective-permute-start(f32[24,512]{1,0:T(8,128)S(1)} %fusion), channel_id=1, source_target_pairs={{0,1},{1,2},{2,3},{3,4},{4,5},{5,6},{6,7},{7,8},{8,9},{9,10},{10,1... | collective-permute-start | bytes 147464
  160.4 27.0 %collective-permute-start.4 = (f32[9,512]{1,0:T(8,128)S(1)}, f32[9,512]{1,0:T(8,128)S(1)}, u32[]{:S(2)}, u32[]{:S(2)}) collective-permute-start(f32[9,512]{1,0:T(8,128)S(1)} %slice.24), channel_id=1, source_target_pairs={{0,5},{1,6},{2,7},{3,8},{4,9},{5,10},{6,11},{7,12},{8,13},{9,14},{... | collective-permute-start | bytes 55304
Sparse Core Ops, SparseCore 0:
  10.5 85.0 all-gather.1
where the time goes:
time: 196 us
  blocking collectives  73.3 us (37%)
  waiting for transfers between devices  44.4 us (23%)
  other arithmetic  33.7 us (17%)
  starting transfers between devices  16.3 us (8%)
  between operations  15.5 us (8%)
  local copies, waits for them, and re-layouts  9.01 us (5%)
  matrix products  3.59 us (2%)
    unnamed x3, blocking collectives  73.3 us
    all_gather x1, waiting for transfers between devices, per_device(): lax.all_gather(masked, 'station', axis=1, tiled=True)  44.4 us
    another operation x4, other arithmetic  20.9 us
    unnamed x5, starting transfers between devices  16.3 us
    all_gather x1, other arithmetic, per_device(): lax.all_gather(masked, 'station', axis=1, tiled=True)  7.73 us
    unnamed x11, local copies, waits for them, and re-layouts  4.29 us
  transfers between devices with their start and end apart: 6, of which 1 were waited for; matrix products, arithmetic and copies ran while one was open for 13% of the time, Pallas kernels for 0%

commit v1 on v0

v1 whole, which is shorter than its diff:
```python
import math

import jax
import jax.numpy as jnp
import numpy as np
from jax import lax
from jax.experimental import pallas as pl
from jax.experimental.pallas import tpu as pltpu
from jax.sharding import PartitionSpec as P

LAGS = 512
NX, NY = 4, 8
NT = 16
SLOTS = 17
ROWS = 17
HALF = 2048
BINS = HALF // NT
TILES = 17
CUT = 9
f32, bf16 = jnp.float32, jnp.bfloat16


def lag_table():
    bins = np.arange(HALF, dtype=np.int64)
    shifts = np.arange(LAGS, dtype=np.int64) - LAGS // 2
    phase = (2 * bins[:, None] + 1) * shifts[None, :] % (4 * HALF)
    angle = phase * (math.pi / (2.0 * HALF))
    table = np.stack([np.cos(angle), -np.sin(angle)]).reshape(2, NT, BINS, LAGS)
    return table.transpose(1, 0, 2, 3).reshape(NT, 2 * BINS, LAGS).astype(bf16)


def kernel(plan, valid, x_ref, table_ref, out_ref,
           msg, got, G, own, stack, recv, tab, pairs,
           tab_sem, s1, r1, say, ray, sax, rax, sbx, rbx, sby, rby, s4, r4):
    st, t = lax.axis_index("station"), lax.axis_index("tm")
    y, x = st // NX, st % NX

    def plane(yy, xx):
        return {"station": (yy % NY) * NX + xx % NX}

    barrier = pltpu.get_barrier_semaphore()
    for j in range(1, NT):
        pl.semaphore_signal(barrier, inc=1, device_id={"tm": (t + j) % NT},
                            device_id_type=pl.DeviceIdType.MESH)
    for j in range(1, NX):
        pl.semaphore_signal(barrier, inc=1, device_id=plane(y, x + j),
                            device_id_type=pl.DeviceIdType.MESH)
    for j in (1, NY - 1):
        pl.semaphore_signal(barrier, inc=1, device_id=plane(y + j, x),
                            device_id_type=pl.DeviceIdType.MESH)

    tab_copy = pltpu.make_async_copy(table_ref, tab, tab_sem)
    tab_copy.start()

    row = lax.broadcasted_iota(jnp.int32, (4, BINS), 0)
    flag = jnp.where(row == 0, valid[0, 0],
                     jnp.where(row == 1, valid[0, 1],
                               jnp.where(row == 2, valid[0, 2], valid[0, 3]))).astype(f32)
    for j in range(NT):
        re = x_ref[0, :, j * BINS:(j + 1) * BINS].astype(f32) * flag
        im = x_ref[0, :, HALF + j * BINS:HALF + (j + 1) * BINS].astype(f32) * flag
        msg[j] = jnp.concatenate([re, im, flag, flag], axis=0).astype(bf16)

    pl.semaphore_wait(barrier, NT - 1 + NX - 1 + 2)

    first = []
    for j in range(1, NT):
        c = pltpu.make_async_remote_copy(
            src_ref=msg.at[(t + j) % NT], dst_ref=got.at[t], send_sem=s1.at[j], recv_sem=r1.at[j],
            device_id={"tm": (t + j) % NT}, device_id_type=pl.DeviceIdType.MESH)
        c.start()
        first.append(c)
    got[t] = msg[t]
    for c in first:
        c.wait_recv()
    lane = lax.broadcasted_iota(jnp.int32, (8, BINS), 1)
    flags = jnp.zeros((8, BINS), f32)
    for h in range(NT):
        tile = got[h].astype(f32)
        G[y, x, h + (1 if h >= CUT - 1 else 0)] = tile[0:8].astype(bf16)
        flags = jnp.where(lane == h, tile[8:16], flags)
        for q in range(8):
            own[h, q] = jnp.broadcast_to(tile[q:q + 1], (8, BINS))
    G[y, x, CUT - 1] = flags.astype(bf16)

    sends = []

    def send(ref, to, ssem, rsem):
        c = pltpu.make_async_remote_copy(src_ref=ref, dst_ref=ref, send_sem=ssem, recv_sem=rsem,
                                         device_id=to, device_id_type=pl.DeviceIdType.MESH)
        c.start()
        sends.append(c)
        return c

    def A(yy, xx):
        return G.at[yy % NY, xx % NX, pl.ds(0, CUT)]

    def B(yy, xx):
        return G.at[yy % NY, xx % NX, pl.ds(CUT, TILES - CUT)]

    def BY(yy):
        return G.at[yy % NY, :, pl.ds(CUT, TILES - CUT)]

    def send_ax(n, yy):
        return [send(A(yy, x), plane(y, x + j), sax.at[n, j], rax.at[n, j]) for j in range(1, NX)]

    bx = [send(B(y, x), plane(y, x + j), sbx.at[j], rbx.at[j]) for j in range(1, NX)]
    up = send(A(y, x), plane(y + 1, x), say.at[0, 0], ray.at[0, 0])
    down = send(A(y, x), plane(y - 1, x), say.at[1, 0], ray.at[1, 0])
    ax = send_ax(0, y)
    for c in bx:
        c.wait_recv()
    bup = send(BY(y), plane(y + 1, x), sby.at[0, 0], rby.at[0, 0])
    bdown = send(BY(y), plane(y - 1, x), sby.at[1, 0], rby.at[1, 0])
    for s in range(1, 5):
        up.wait_recv()
        if s < 4:
            down.wait_recv()
            up = send(A(y - s, x), plane(y + 1, x), say.at[0, s], ray.at[0, s])
            if s < 3:
                down = send(A(y + s, x), plane(y - 1, x), say.at[1, s], ray.at[1, s])
        ax += send_ax(2 * s - 1, y - s)
        if s < 4:
            ax += send_ax(2 * s, y + s)
        bdown.wait_recv()
        if s < 4:
            bup.wait_recv()
            bdown = send(BY(y + s), plane(y - 1, x), sby.at[1, s], rby.at[1, s])
            if s < 3:
                bup = send(BY(y - s), plane(y + 1, x), sby.at[0, s], rby.at[0, s])
    for c in ax:
        c.wait_recv()

    top = lax.broadcasted_iota(jnp.int32, (8, BINS), 0) < 4

    def slots(ks):
        tiles = []
        for k in ks:
            blk = plan[0, k]
            tiles.append((blk // NX, blk % NX))
        acc = [[[None, None] for _ in range(4)] for _ in ks]
        for h in range(NT):
            g = [G[by, bx_, h + (1 if h >= CUT - 1 else 0)].astype(f32) for by, bx_ in tiles]
            for a in range(4):
                for c in range(2):
                    o = own[h, 4 * c + a]
                    for n in range(len(ks)):
                        p = o * g[n]
                        acc[n][a][c] = p if h == 0 else acc[n][a][c] + p
        for n, k in enumerate(ks):
            for half in range(2):
                (e1, e2), (o1, o2) = acc[n][2 * half], acc[n][2 * half + 1]
                roll = lambda v: pltpu.roll(v, 4, 0)
                re = jnp.where(top, e1 + roll(e2), roll(o1) + o2)
                im = jnp.where(top, e2 - roll(e1), roll(o2) - o1)
                stack[2 * k + half, :, 0:BINS] = re.astype(bf16)
                stack[2 * k + half, :, BINS:2 * BINS] = im.astype(bf16)
            by, bx_ = tiles[n]
            fl = G[by, bx_, CUT - 1].astype(f32)
            of = G[y, x, CUT - 1].astype(f32)
            fe = jnp.where(top, fl, pltpu.roll(fl, 4, 0))
            for half in range(2):
                oa = jnp.where(top, jnp.broadcast_to(of[2 * half:2 * half + 1], (8, BINS)),
                               jnp.broadcast_to(of[2 * half + 1:2 * half + 2], (8, BINS)))
                pairs[2 * k + half] = fe * oa

    slots([0])

    def two(i, carry):
        slots([2 * i + 1, 2 * i + 2])
        return carry

    lax.fori_loop(0, 8, two, 0)

    last = []
    for j in range(1, NT):
        to = (t + j) % NT
        c = pltpu.make_async_remote_copy(
            src_ref=stack.at[pl.ds(ROWS * to // 8, 3)], dst_ref=recv.at[t],
            send_sem=s4.at[j], recv_sem=r4.at[j],
            device_id={"tm": to}, device_id_type=pl.DeviceIdType.MESH)
        c.start()
        last.append(c)
    base = ROWS * t // 8
    mine = jnp.concatenate([stack[base + i].astype(f32) for i in range(3)], axis=0).astype(bf16)
    counts = jnp.concatenate(
        [jnp.sum(pairs[base + i], axis=1, keepdims=True) for i in range(3)], axis=0)
    tab_copy.wait()
    acc = jnp.dot(mine, tab[t], preferred_element_type=f32)
    for j in range(1, NT):
        last[j - 1].wait_recv()
        src = (t + NT - j) % NT
        lhs = jnp.concatenate([recv[src, i].astype(f32) for i in range(3)], axis=0).astype(bf16)
        acc = acc + jnp.dot(lhs, tab[src], preferred_element_type=f32)
    res = acc * (4.0 / math.sqrt(HALF)) / counts
    shift = ROWS * t % 8
    res = pltpu.roll(res, (24 - shift) % 24, 0)
    out_ref[...] = res[0:ROWS]
    for c in first + sends + last:
        c.wait_send()


def per_device(spectra, valid, pair_blocks):
    dma = pltpu.SemaphoreType.DMA
    vmem = pl.BlockSpec(memory_space=pltpu.VMEM)
    smem = pl.BlockSpec(memory_space=pltpu.SMEM)
    return pl.pallas_call(
        kernel,
        out_shape=jax.ShapeDtypeStruct((ROWS, LAGS), f32),
        in_specs=[smem, smem, vmem, pl.BlockSpec(memory_space=pl.ANY)],
        out_specs=vmem,
        scratch_shapes=[
            pltpu.VMEM((NT, 16, BINS), bf16),
            pltpu.VMEM((NT, 16, BINS), bf16),
            pltpu.VMEM((NY, NX, TILES, 8, BINS), bf16),
            pltpu.VMEM((NT, 8, 8, BINS), f32),
            pltpu.VMEM((2 * SLOTS, 8, 2 * BINS), bf16),
            pltpu.VMEM((NT, 3, 8, 2 * BINS), bf16),
            pltpu.VMEM((NT, 2 * BINS, LAGS), bf16),
            pltpu.VMEM((2 * SLOTS, 8, BINS), f32),
            dma, dma((NT,)), dma((NT,)), dma((2, 4)), dma((2, 4)),
            dma((NY, NX)), dma((NY, NX)), dma((NX,)), dma((NX,)),
            dma((2, 4)), dma((2, 4)), dma((NT,)), dma((NT,)),
        ],
        compiler_params=pltpu.CompilerParams(
            collective_id=0, has_side_effects=True, vmem_limit_bytes=24 << 20),
    )(pair_blocks, valid, spectra, jnp.asarray(lag_table()))


def solution(mesh):
    placed = (P("tm", "station", None), P("tm", "station"), P("station", None))
    return jax.shard_map(
        per_device,
        mesh=mesh,
        in_specs=placed,
        out_specs=P(("station", "tm"), None),
        check_vma=False,
    )
```

time: 196 us -> 53.6 us (0.27)
  blocking collectives: 73.3 us -> 0 us
  Pallas kernels: 0 us -> 48.5 us
  waiting for transfers between devices: 44.4 us -> 0 us
  other arithmetic: 33.7 us -> 0 us
  starting transfers between devices: 16.3 us -> 0 us
  between operations: 15.5 us -> 0.01 us
  local copies, waits for them, and re-layouts: 9.01 us -> 4.88 us
  matrix products: 3.59 us -> 0 us
    unnamed x3 -> x0, blocking collectives: 73.3 us -> none
    pallas_call x0 -> x1, Pallas kernels: none -> 48.5 us  [per_device(): pl.pallas_call(kernel, out_shape=jax.ShapeDtypeStruct((ROWS, LAGS), f32),...]
    all_gather x1 -> x0, waiting for transfers between devices: 44.4 us -> none  [per_device(): lax.all_gather(masked, 'station', axis=1, tiled=True)]
    another operation x4 -> x0, other arithmetic: 20.9 us -> none
    unnamed x5 -> x0, starting transfers between devices: 16.3 us -> none
    all_gather x1 -> x0, other arithmetic: 7.73 us -> none  [per_device(): lax.all_gather(masked, 'station', axis=1, tiled=True)]
    dot_general x1 -> x0, matrix products: 3.59 us -> none  [per_device(): jnp.dot(stacked, lag_table, preferred_element_type=jnp.float32)]
    concatenate x2 -> x0, local copies, waits for them, and re-layouts: 2.28 us -> none  [cross_stack(): jnp.concatenate([cross_real, cross_imag], axis=-1).astype(jnp.bfloat16)]
  transfers between devices with their start and end apart: 6 -> 0, of which waited for: 1 -> 0; matrix products, arithmetic and copies ran while one was open for 13% -> 0% of each run, Pallas kernels for 0% -> 0%
where the time goes in v1:
time: 53.6 us; the launch traced here: 53.4 us
  Pallas kernels  48.5 us (90%)
  local copies, waits for them, and re-layouts  4.88 us (9%)
    pallas_call x1, Pallas kernels, per_device(): pl.pallas_call(kernel, out_shape=jax.ShapeDtypeStruct((ROWS, LAGS), f32),...  48.5 us
    unnamed x9, local copies, waits for them, and re-layouts  4.88 us

profile of v1, /device:TPU:1, one launch (start us, length us, event | category | flops | bytes accessed | tf_op | source)
XLA Modules:
  0.0 53.4 jit_solution(688514575383316783)
XLA Ops:
  0.0 0.0 copy-start
  0.0 2.2 %copy-done = bf16[16,256,512]{2,1,0:T(8,128)(2,1)S(1)} copy-done((bf16[16,256,512]{2,1,0:T(8,128)(2,1)S(1)}, bf16[16,256,512]{2,1,0:T(8,128)(2,1)}, u32[]{:S(2)}) %copy-start) | copy-done | bytes 4194328
  2.2 0.0 copy-start.1
  2.2 0.8 %copy-done.1 = bf16[1,4,4096]{2,1,0:T(4,128)(2,1)S(1)} copy-done((bf16[1,4,4096]{2,1,0:T(4,128)(2,1)S(1)}, bf16[1,4,4096]{2,1,0:T(4,128)(2,1)}, u32[]{:S(2)}) %copy-start.1) | copy-done | bytes 32792
  2.9 0.0 copy-start.2
  2.9 0.7 %copy-done.2 = s32[1,17]{1,0:T(1,128)S(1)} copy-done((s32[1,17]{1,0:T(1,128)S(1)}, s32[1,17]{1,0:T(1,128)}, u32[]{:S(2)}) %copy-start.2) | copy-done | bytes 92
  3.6 0.0 copy-start.3
  3.6 0.7 %copy-done.3 = s32[1,4]{1,0:T(1,128)S(1)} copy-done((s32[1,4]{1,0:T(1,128)S(1)}, s32[1,4]{1,0:T(1,128)}, u32[]{:S(2)}) %copy-start.3) | copy-done | bytes 40
  4.3 48.5 %shard_map.46 = f32[17,512]{1,0:T(8,128)S(1)} custom-call(s32[1,17]{1,0:T(1,128)S(1)} %copy-done.2, s32[1,4]{1,0:T(1,128)S(1)} %copy-done.3, bf16[1,4,4096]{2,1,0:T(4,128)(2,1)S(1)} %copy-done.1, bf16[16,256,512]{2,1,0:T(8,128)(2,1)S(1)} %copy-done), custom_call_target="tpu_custom_call" | custom-call | tf_op jit(solution)/shard_map/pallas_call | solution.py:207
  52.7 0.6 %copy.6 = f32[17,512]{1,0:T(8,128)} copy(f32[17,512]{1,0:T(8,128)S(1)} %shard_map.46) | data formatting | bytes 69632
Async XLA Ops:
  0.0 2.2 %copy-start = (bf16[16,256,512]{2,1,0:T(8,128)(2,1)S(1)}, bf16[16,256,512]{2,1,0:T(8,128)(2,1)}, u32[]{:S(2)}) copy-start(bf16[16,256,512]{2,1,0:T(8,128)(2,1)} %constant.2.clone.table_ref) | copy-start | bytes 12582916
  2.2 0.8 %copy-start.1 = (bf16[1,4,4096]{2,1,0:T(4,128)(2,1)S(1)}, bf16[1,4,4096]{2,1,0:T(4,128)(2,1)}, u32[]{:S(2)}) copy-start(bf16[1,4,4096]{2,1,0:T(4,128)(2,1)} %x_ref.1) | copy-start | bytes 98308
  2.9 0.7 %copy-start.2 = (s32[1,17]{1,0:T(1,128)S(1)}, s32[1,17]{1,0:T(1,128)}, u32[]{:S(2)}) copy-start(s32[1,17]{1,0:T(1,128)} %plan.1) | copy-start | bytes 208
  3.6 0.7 %copy-start.3 = (s32[1,4]{1,0:T(1,128)S(1)}, s32[1,4]{1,0:T(1,128)}, u32[]{:S(2)}) copy-start(s32[1,4]{1,0:T(1,128)} %valid.1) | copy-start | bytes 52

commit v2 on v1

--- a/solution.py
+++ b/solution.py
@@ -20,23 +20,33 @@
 f32, bf16 = jnp.float32, jnp.bfloat16
 
 
-def lag_table():
-    bins = np.arange(HALF, dtype=np.int64)
+def lag_base():
     shifts = np.arange(LAGS, dtype=np.int64) - LAGS // 2
-    phase = (2 * bins[:, None] + 1) * shifts[None, :] % (4 * HALF)
-    angle = phase * (math.pi / (2.0 * HALF))
-    table = np.stack([np.cos(angle), -np.sin(angle)]).reshape(2, NT, BINS, LAGS)
-    return table.transpose(1, 0, 2, 3).reshape(NT, 2 * BINS, LAGS).astype(bf16)
-
-
-def kernel(plan, valid, x_ref, table_ref, out_ref,
-           msg, got, G, own, stack, recv, tab, pairs,
-           tab_sem, s1, r1, say, ray, sax, rax, sbx, rbx, sby, rby, s4, r4):
+    unit = math.pi / (2.0 * HALF)
+
+    def both(steps):
+        angle = steps[:, None] * shifts[None, :] % (4 * HALF) * unit
+        return np.stack([np.cos(angle), np.sin(angle)]).astype(np.float32)
+
+    base = both(2 * np.arange(BINS, dtype=np.int64) + 1)
+    turn = both(2 * BINS * np.arange(NT, dtype=np.int64))
+    return base, turn
+
+
+def kernel(plan_ref, valid_ref, spectra_ref, base_ref, turn_ref, out_ref,
+           plan, valid, x_ref, base, turn, msg, got, G, own, stack, recv, tab, pairs,
+           in_sem, s1, r1, say, ray, sax, rax, sbx, rbx, sby, rby, s4, r4):
     st, t = lax.axis_index("station"), lax.axis_index("tm")
     y, x = st // NX, st % NX
 
     def plane(yy, xx):
         return {"station": (yy % NY) * NX + xx % NX}
+
+    loads = [pltpu.make_async_copy(a, b, in_sem.at[i]) for i, (a, b) in enumerate(
+        [(spectra_ref, x_ref), (valid_ref, valid), (plan_ref, plan), (base_ref, base),
+         (turn_ref, turn)])]
+    for c in loads:
+        c.start()
 
     barrier = pltpu.get_barrier_semaphore()
     for j in range(1, NT):
@@ -49,9 +59,8 @@
         pl.semaphore_signal(barrier, inc=1, device_id=plane(y + j, x),
                             device_id_type=pl.DeviceIdType.MESH)
 
-    tab_copy = pltpu.make_async_copy(table_ref, tab, tab_sem)
-    tab_copy.start()
-
+    loads[0].wait()
+    loads[1].wait()
     row = lax.broadcasted_iota(jnp.int32, (4, BINS), 0)
     flag = jnp.where(row == 0, valid[0, 0],
                      jnp.where(row == 1, valid[0, 1],
@@ -71,6 +80,20 @@
         c.start()
         first.append(c)
     got[t] = msg[t]
+
+    for c in loads[2:]:
+        c.wait()
+
+    def fill(j, carry):
+        tc = turn[0, pl.ds(j, 1), :]
+        ts = turn[1, pl.ds(j, 1), :]
+        for i in range(0, BINS, 16):
+            bc, bs = base[0, i:i + 16], base[1, i:i + 16]
+            tab[j, i:i + 16] = (bc * tc - bs * ts).astype(bf16)
+            tab[j, BINS + i:BINS + i + 16] = (-(bs * tc + bc * ts)).astype(bf16)
+        return carry
+
+    lax.fori_loop(0, NT, fill, 0)
     for c in first:
         c.wait_recv()
     lane = lax.broadcasted_iota(jnp.int32, (8, BINS), 1)
@@ -185,7 +208,6 @@
     mine = jnp.concatenate([stack[base + i].astype(f32) for i in range(3)], axis=0).astype(bf16)
     counts = jnp.concatenate(
         [jnp.sum(pairs[base + i], axis=1, keepdims=True) for i in range(3)], axis=0)
-    tab_copy.wait()
     acc = jnp.dot(mine, tab[t], preferred_element_type=f32)
     for j in range(1, NT):
         last[j - 1].wait_recv()
@@ -202,14 +224,19 @@
 
 def per_device(spectra, valid, pair_blocks):
     dma = pltpu.SemaphoreType.DMA
-    vmem = pl.BlockSpec(memory_space=pltpu.VMEM)
-    smem = pl.BlockSpec(memory_space=pltpu.SMEM)
+    anywhere = pl.BlockSpec(memory_space=pl.ANY)
+    base, turn = lag_base()
     return pl.pallas_call(
         kernel,
         out_shape=jax.ShapeDtypeStruct((ROWS, LAGS), f32),
-        in_specs=[smem, smem, vmem, pl.BlockSpec(memory_space=pl.ANY)],
-        out_specs=vmem,
+        in_specs=[anywhere] * 5,
+        out_specs=pl.BlockSpec(memory_space=pltpu.VMEM),
         scratch_shapes=[
+            pltpu.SMEM((1, SLOTS), jnp.int32),
+            pltpu.SMEM((1, 4), jnp.int32),
+            pltpu.VMEM((1, 4, 2 * HALF), bf16),
+            pltpu.VMEM((2, BINS, LAGS), f32),
+            pltpu.VMEM((2, NT, LAGS), f32),
             pltpu.VMEM((NT, 16, BINS), bf16),
             pltpu.VMEM((NT, 16, BINS), bf16),
             pltpu.VMEM((NY, NX, TILES, 8, BINS), bf16),
@@ -218,13 +245,13 @@
             pltpu.VMEM((NT, 3, 8, 2 * BINS), bf16),
             pltpu.VMEM((NT, 2 * BINS, LAGS), bf16),
             pltpu.VMEM((2 * SLOTS, 8, BINS), f32),
-            dma, dma((NT,)), dma((NT,)), dma((2, 4)), dma((2, 4)),
+            dma((5,)), dma((NT,)), dma((NT,)), dma((2, 4)), dma((2, 4)),
             dma((NY, NX)), dma((NY, NX)), dma((NX,)), dma((NX,)),
             dma((2, 4)), dma((2, 4)), dma((NT,)), dma((NT,)),
         ],
         compiler_params=pltpu.CompilerParams(
-            collective_id=0, has_side_effects=True, vmem_limit_bytes=24 << 20),
-    )(pair_blocks, valid, spectra, jnp.asarray(lag_table()))
+            collective_id=0, has_side_effects=True, vmem_limit_bytes=60 << 20),
+    )(pair_blocks, valid, spectra, jnp.asarray(base), jnp.asarray(turn))
 
 
 def solution(mesh):

time: 53.6 us -> 50.2 us (0.937)
  local copies, waits for them, and re-layouts: 4.88 us -> 1.42 us
    unnamed x9 -> x1, local copies, waits for them, and re-layouts: 4.88 us -> 1.42 us
where the time goes in v2:
time: 50.2 us; the launch traced here: 50 us
  Pallas kernels  48.6 us (97%)
  local copies, waits for them, and re-layouts  1.42 us (3%)
    pallas_call x1, Pallas kernels, per_device(): pl.pallas_call(kernel, out_shape=jax.ShapeDtypeStruct((ROWS, LAGS), f32),...  48.6 us
    unnamed x1, local copies, waits for them, and re-layouts  1.42 us

profile of v2, /device:TPU:1, one launch (start us, length us, event | category | flops | bytes accessed | tf_op | source)
XLA Modules:
  0.0 50.0 jit_solution(8100147232498109727)
XLA Ops:
  0.0 48.6 %shard_map.55 = f32[17,512]{1,0:T(8,128)} custom-call(s32[1,17]{1,0:T(1,128)} %plan_ref.1, s32[1,4]{1,0:T(1,128)} %valid_ref.1, bf16[1,4,4096]{2,1,0:T(4,128)(2,1)} %spectra_ref.1, f32[2,128,512]{2,1,0:T(8,128)} %constant.4.clone.base_ref, f32[2,16,512]{2,1,0:T(8,128)} %constant.5.clone.turn_ref), custom_call_target="tpu_custom_call" | custom-call | tf_op jit(solution)/shard_map/pallas_call | solution.py:229
  48.6 1.4 %copy.7 = f32[17,512]{1,0:T(8,128)} copy(f32[17,512]{1,0:T(8,128)} %shard_map.55) | data formatting | bytes 69632

commit v3 on v2

v3 whole, which is shorter than its diff:
```python
import math

import jax
import jax.numpy as jnp
import numpy as np
from jax import lax
from jax.experimental import pallas as pl
from jax.experimental.pallas import tpu as pltpu
from jax.sharding import PartitionSpec as P

LAGS = 512
NX, NY = 4, 8
NT = 16
SLOTS = 17
ROWS = 17
HALF = 2048
BINS = HALF // NT
TILES = 17
CUT = 12
DIST = (0, 1, 7, 2, 6, 3, 5, 4)
PEERS = [(dz, dc) for dz in DIST for dc in (0, 1)][1:]
HOP = (1, NY - 1, 2, NY - 2, 1, NY - 1, 2, NY - 2)
f32, bf16 = jnp.float32, jnp.bfloat16


def lag_base():
    shifts = np.arange(LAGS, dtype=np.int64) - LAGS // 2
    unit = math.pi / (2.0 * HALF)

    def both(steps):
        angle = steps[:, None] * shifts[None, :] % (4 * HALF) * unit
        return np.stack([np.cos(angle), np.sin(angle)]).astype(np.float32)

    base = both(2 * np.arange(BINS, dtype=np.int64) + 1)
    turn = both(2 * BINS * np.arange(NT, dtype=np.int64))
    return base, turn


def kernel(plan_ref, valid_ref, spectra_ref, base_ref, turn_ref, out_ref,
           plan, valid, x_ref, base, turn, msg, got, G, own, stack, recv, tab, pairs,
           in_sem, s1, r1, say, ray, sax, rax, sbx, rbx, sby, rby, s4, r4):
    st, t = lax.axis_index("station"), lax.axis_index("tm")
    y, x = st // NX, st % NX
    z, core = t // 2, t % 2

    def line(dz, dc):
        return (z + dz) % 8 * 2 + (core + dc) % 2

    def slot(dz, dc):
        return 2 * DIST.index(dz % 8) + dc

    def tile(n):
        return n if n < CUT else n + 1

    def plane(yy, xx):
        return {"station": (yy % NY) * NX + xx % NX}

    loads = [pltpu.make_async_copy(a, b, in_sem.at[i]) for i, (a, b) in enumerate(
        [(spectra_ref, x_ref), (valid_ref, valid), (plan_ref, plan), (base_ref, base),
         (turn_ref, turn)])]
    for c in loads:
        c.start()

    barrier = pltpu.get_barrier_semaphore()
    for p in reversed(PEERS):
        pl.semaphore_signal(barrier, inc=1, device_id={"tm": line(*p)},
                            device_id_type=pl.DeviceIdType.MESH)
    for j in range(1, NX):
        pl.semaphore_signal(barrier, inc=1, device_id=plane(y, x + j),
                            device_id_type=pl.DeviceIdType.MESH)
    for j in (1, 2, NY - 2, NY - 1):
        pl.semaphore_signal(barrier, inc=1, device_id=plane(y + j, x),
                            device_id_type=pl.DeviceIdType.MESH)

    loads[0].wait()
    loads[1].wait()
    row = lax.broadcasted_iota(jnp.int32, (4, BINS), 0)
    flag = jnp.where(row == 0, valid[0, 0],
                     jnp.where(row == 1, valid[0, 1],
                               jnp.where(row == 2, valid[0, 2], valid[0, 3]))).astype(f32)
    for j in range(NT):
        re = x_ref[0, :, j * BINS:(j + 1) * BINS].astype(f32) * flag
        im = x_ref[0, :, HALF + j * BINS:HALF + (j + 1) * BINS].astype(f32) * flag
        msg[j] = jnp.concatenate([re, im, flag, flag], axis=0).astype(bf16)

    pl.semaphore_wait(barrier, NT - 1 + NX - 1 + 4)

    first = {}
    for dz, dc in reversed(PEERS):
        to = line(dz, dc)
        c = pltpu.make_async_remote_copy(
            src_ref=msg.at[to], dst_ref=got.at[slot(-dz, dc)], send_sem=s1.at[slot(-dz, dc)],
            recv_sem=r1.at[slot(-dz, dc)], device_id={"tm": to},
            device_id_type=pl.DeviceIdType.MESH)
        c.start()
        first[slot(-dz, dc)] = c
    got[0] = msg[t]

    for c in loads[2:]:
        c.wait()

    def fill(j, carry):
        tc = turn[0, pl.ds(j, 1), :]
        ts = turn[1, pl.ds(j, 1), :]
        for i in range(0, BINS, 16):
            bc, bs = base[0, i:i + 16], base[1, i:i + 16]
            tab[j, i:i + 16] = (bc * tc - bs * ts).astype(bf16)
            tab[j, BINS + i:BINS + i + 16] = (-(bs * tc + bc * ts)).astype(bf16)
        return carry

    lax.fori_loop(0, NT, fill, 0)
    sends = []

    def send(ref, to, ssem, rsem):
        c = pltpu.make_async_remote_copy(src_ref=ref, dst_ref=ref, send_sem=ssem, recv_sem=rsem,
                                         device_id=to, device_id_type=pl.DeviceIdType.MESH)
        c.start()
        sends.append(c)
        return c

    def A(yy, xx):
        return G.at[yy % NY, xx % NX, pl.ds(0, CUT)]

    def B(yy, xx):
        return G.at[yy % NY, xx % NX, pl.ds(CUT, TILES - CUT)]

    def BY(yy):
        return G.at[yy % NY, :, pl.ds(CUT, TILES - CUT)]

    def send_ax(n, yy):
        return [send(A(yy, x), plane(y, x + j), sax.at[n, j], rax.at[n, j]) for j in range(1, NX)]

    def far(block, n, ssem, rsem):
        return send(block, plane(y + HOP[n], x), ssem.at[n], rsem.at[n])

    def relay(block, half, ssem, rsem):
        return [far(block(y - 2), 4, ssem, rsem), far(block(y + 2), 5, ssem, rsem),
                far(half(y - 2, 0), 6, ssem, rsem), far(half(y + 2, 1), 7, ssem, rsem)]

    def A_half(yy, h):
        return G.at[yy % NY, x, pl.ds(h * (CUT // 2), CUT // 2 if h == 0 else CUT - CUT // 2)]

    def B_half(yy, h):
        n = TILES - CUT
        return G.at[yy % NY, :, pl.ds(CUT + h * (n // 2), n // 2 if h == 0 else n - n // 2)]

    def arrive(n):
        if n > 0:
            first[n].wait_recv()
        G[y, x, tile(n)] = got[n, 0:8]

    for n in range(CUT):
        arrive(n)
    ay = [far(A(y, x), n, say, ray) for n in (0, 1, 2, 3)]
    for n in range(CUT, NT):
        arrive(n)
    lane = lax.broadcasted_iota(jnp.int32, (8, BINS), 1)
    flags = jnp.zeros((8, BINS), f32)
    for n in range(NT):
        flags = jnp.where(lane == n, got[n, 8:16].astype(f32), flags)
    G[y, x, CUT] = flags.astype(bf16)
    bx = [send(B(y, x), plane(y, x + j), sbx.at[j], rbx.at[j]) for j in range(1, NX)]
    ax = send_ax(0, y)
    for n in range(NT):
        mine = got[n, 0:8].astype(f32)
        for q in range(8):
            own[n, q] = jnp.broadcast_to(mine[q:q + 1], (8, BINS))
    for c in bx:
        c.wait_recv()
    by = [far(BY(y), n, sby, rby) for n in range(4)]
    ay[2].wait_recv()
    ay[3].wait_recv()
    ay += relay(lambda yy: A(yy, x), A_half, say, ray)
    ay[0].wait_recv()
    ax += send_ax(1, y - 1)
    ay[1].wait_recv()
    ax += send_ax(2, y + 1)
    ax += send_ax(3, y - 2)
    ax += send_ax(4, y + 2)
    by[2].wait_recv()
    by[3].wait_recv()
    by += relay(BY, B_half, sby, rby)
    ay[4].wait_recv()
    ax += send_ax(5, y - 3)
    ay[5].wait_recv()
    ax += send_ax(6, y + 3)
    ay[6].wait_recv()
    ay[7].wait_recv()
    ax += send_ax(7, y + 4)
    for c in by[:2] + by[4:] + ax:
        c.wait_recv()

    top = lax.broadcasted_iota(jnp.int32, (8, BINS), 0) < 4

    def slots(ks):
        tiles = []
        for k in ks:
            blk = plan[0, k]
            tiles.append((blk // NX, blk % NX))
        acc = [[[None, None] for _ in range(4)] for _ in ks]
        for h in range(NT):
            g = [G[by, bx_, tile(h)].astype(f32) for by, bx_ in tiles]
            for a in range(4):
                for c in range(2):
                    o = own[h, 4 * c + a]
                    for n in range(len(ks)):
                        p = o * g[n]
                        acc[n][a][c] = p if h == 0 else acc[n][a][c] + p
        for n, k in enumerate(ks):
            for a in range(4):
                p, q = acc[n][a]
                re = p + pltpu.roll(q, 4, 0)
                im = q - pltpu.roll(p, 4, 0)
                stack[4 * k + a, :, 0:BINS] = re[0:4].astype(bf16)
                stack[4 * k + a, :, BINS:2 * BINS] = im[0:4].astype(bf16)
            by, bx_ = tiles[n]
            fl = G[by, bx_, CUT].astype(f32)
            of = G[y, x, CUT].astype(f32)
            fe = jnp.where(top, fl, pltpu.roll(fl, 4, 0))
            for half in range(2):
                oa = jnp.where(top, jnp.broadcast_to(of[2 * half:2 * half + 1], (8, BINS)),
                               jnp.broadcast_to(of[2 * half + 1:2 * half + 2], (8, BINS)))
                pairs[2 * k + half] = fe * oa

    slots([0])

    def two(i, carry):
        slots([2 * i + 1, 2 * i + 2])
        return carry

    lax.fori_loop(0, 8, two, 0)

    last = {}
    for dz, dc in reversed(PEERS):
        to = line(dz, dc)
        c = pltpu.make_async_remote_copy(
            src_ref=stack.at[pl.ds(ROWS * to // 4, 5)], dst_ref=recv.at[slot(-dz, dc)],
            send_sem=s4.at[slot(-dz, dc)], recv_sem=r4.at[slot(-dz, dc)],
            device_id={"tm": to}, device_id_type=pl.DeviceIdType.MESH)
        c.start()
        last[slot(-dz, dc)] = c
    def rows(read):
        pad = jnp.zeros((4, 2 * BINS), f32)
        return jnp.concatenate([read(i).astype(f32) for i in range(5)] + [pad], axis=0).astype(bf16)

    def align(v, shift):
        return pltpu.roll(v, (24 - shift) % 24, 0)[0:ROWS]

    first_row = ROWS * t // 8
    counts = jnp.concatenate([pairs[first_row + i] for i in range(3)], axis=0)
    counts = align(jnp.broadcast_to(jnp.sum(counts, axis=1, keepdims=True), (24, BINS)), ROWS * t % 8)
    gain = jnp.concatenate([(4.0 / math.sqrt(HALF)) / counts] * (LAGS // BINS), axis=1)
    first_row = ROWS * t // 4
    mine = rows(lambda i: stack[first_row + i])
    acc = jnp.dot(mine, tab[t], preferred_element_type=f32)
    for dz, dc in PEERS:
        n = slot(dz, dc)
        last[n].wait_recv()
        lhs = rows(lambda i: recv[n, i])
        acc = acc + jnp.dot(lhs, tab[line(dz, dc)], preferred_element_type=f32)
    out_ref[...] = align(acc, ROWS * t % 4) * gain
    for c in list(first.values()) + sends + list(last.values()):
        c.wait_send()


def per_device(spectra, valid, pair_blocks):
    dma = pltpu.SemaphoreType.DMA
    hbm = pl.BlockSpec(memory_space=pltpu.HBM)
    base, turn = lag_base()
    return pl.pallas_call(
        kernel,
        out_shape=jax.ShapeDtypeStruct((ROWS, LAGS), f32),
        in_specs=[hbm] * 5,
        out_specs=pl.BlockSpec(memory_space=pltpu.VMEM),
        scratch_shapes=[
            pltpu.SMEM((1, SLOTS), jnp.int32),
            pltpu.SMEM((1, 4), jnp.int32),
            pltpu.VMEM((1, 4, 2 * HALF), bf16),
            pltpu.VMEM((2, BINS, LAGS), f32),
            pltpu.VMEM((2, NT, LAGS), f32),
            pltpu.VMEM((NT, 16, BINS), bf16),
            pltpu.VMEM((NT, 16, BINS), bf16),
            pltpu.VMEM((NY, NX, TILES, 8, BINS), bf16),
            pltpu.VMEM((NT, 8, 8, BINS), f32),
            pltpu.VMEM((4 * SLOTS, 4, 2 * BINS), bf16),
            pltpu.VMEM((NT, 5, 4, 2 * BINS), bf16),
            pltpu.VMEM((NT, 2 * BINS, LAGS), bf16),
            pltpu.VMEM((2 * SLOTS, 8, BINS), f32),
            dma((5,)), dma((NT,)), dma((NT,)), dma((8,)), dma((8,)),
            dma((NY, NX)), dma((NY, NX)), dma((NX,)), dma((NX,)),
            dma((8,)), dma((8,)), dma((NT,)), dma((NT,)),
        ],
        compiler_params=pltpu.CompilerParams(
            collective_id=0, has_side_effects=True, vmem_limit_bytes=24 << 20),
    )(*[pltpu.with_memory_space_constraint(a, pltpu.HBM) for a in
        (pair_blocks, valid, spectra, jnp.asarray(base), jnp.asarray(turn))])


def solution(mesh):
    placed = (P("tm", "station", None), P("tm", "station"), P("station", None))
    return jax.shard_map(
        per_device,
        mesh=mesh,
        in_specs=placed,
        out_specs=P(("station", "tm"), None),
        check_vma=False,
    )
```

time: 50.2 us -> 42.3 us (0.84)
  Pallas kernels: 48.6 us -> 41.5 us
  local copies, waits for them, and re-layouts: 1.42 us -> 0.62 us
    pallas_call x1, Pallas kernels: 48.6 us -> 41.5 us  [per_device(): pl.pallas_call(kernel, out_shape=jax.ShapeDtypeStruct((ROWS, LAGS), f32),...]
    unnamed x1, local copies, waits for them, and re-layouts: 1.42 us -> 0.62 us
where the time goes in v3:
time: 42.3 us; the launch traced here: 42.2 us
  Pallas kernels  41.5 us (98%)
  local copies, waits for them, and re-layouts  0.62 us (1%)
    pallas_call x1, Pallas kernels, per_device(): pl.pallas_call(kernel, out_shape=jax.ShapeDtypeStruct((ROWS, LAGS), f32),...  41.5 us

profile of v3, /device:TPU:1, one launch (start us, length us, event | category | flops | bytes accessed | tf_op | source)
XLA Modules:
  0.0 42.2 jit_solution(13887057594607245665)
XLA Ops:
  0.0 41.5 %shard_map.55 = f32[17,512]{1,0:T(8,128)S(1)} custom-call(s32[1,17]{1,0:T(1,128)} %plan_ref.1, s32[1,4]{1,0:T(1,128)} %valid_ref.1, bf16[1,4,4096]{2,1,0:T(4,128)(2,1)} %spectra_ref.1, f32[2,128,512]{2,1,0:T(8,128)} %constant.4.clone.base_ref, f32[2,16,512]{2,1,0:T(8,128)} %constant.5.clone.turn_ref), custom_call_target="tpu_custom_call" | custom-call | tf_op jit(solution)/shard_map/pallas_call | solution.py:270
  41.5 0.6 %copy.7 = f32[17,512]{1,0:T(8,128)} copy(f32[17,512]{1,0:T(8,128)S(1)} %shard_map.55) | data formatting | bytes 69632

commit v4 on v3

--- a/solution.py
+++ b/solution.py
@@ -16,8 +16,9 @@
 HALF = 2048
 BINS = HALF // NT
 TILES = 17
-CUT = 12
+CUT = 13
 DIST = (0, 1, 7, 2, 6, 3, 5, 4)
+ORDER = (4, 5, 3, 6, 2, 7, 1, 0)
 PEERS = [(dz, dc) for dz in DIST for dc in (0, 1)][1:]
 HOP = (1, NY - 1, 2, NY - 2, 1, NY - 1, 2, NY - 2)
 f32, bf16 = jnp.float32, jnp.bfloat16
@@ -128,14 +129,14 @@
         return G.at[yy % NY, :, pl.ds(CUT, TILES - CUT)]
 
     def send_ax(n, yy):
-        return [send(A(yy, x), plane(y, x + j), sax.at[n, j], rax.at[n, j]) for j in range(1, NX)]
+        return [send(A(yy, x), plane(y, x + j), sax.at[n, j], rax.at[n, j]) for j in (2, 1, 3)]
 
     def far(block, n, ssem, rsem):
         return send(block, plane(y + HOP[n], x), ssem.at[n], rsem.at[n])
 
     def relay(block, half, ssem, rsem):
-        return [far(block(y - 2), 4, ssem, rsem), far(block(y + 2), 5, ssem, rsem),
-                far(half(y - 2, 0), 6, ssem, rsem), far(half(y + 2, 1), 7, ssem, rsem)]
+        return [far(half(y - 2, 0), 6, ssem, rsem), far(half(y + 2, 1), 7, ssem, rsem),
+                far(block(y - 2), 4, ssem, rsem), far(block(y + 2), 5, ssem, rsem)]
 
     def A_half(yy, h):
         return G.at[yy % NY, x, pl.ds(h * (CUT // 2), CUT // 2 if h == 0 else CUT - CUT // 2)]
@@ -151,7 +152,7 @@
 
     for n in range(CUT):
         arrive(n)
-    ay = [far(A(y, x), n, say, ray) for n in (0, 1, 2, 3)]
+    ay = [far(A(y, x), n, say, ray) for n in (2, 3, 0, 1)]
     for n in range(CUT, NT):
         arrive(n)
     lane = lax.broadcasted_iota(jnp.int32, (8, BINS), 1)
@@ -167,78 +168,84 @@
             own[n, q] = jnp.broadcast_to(mine[q:q + 1], (8, BINS))
     for c in bx:
         c.wait_recv()
-    by = [far(BY(y), n, sby, rby) for n in range(4)]
+    by = [far(BY(y), n, sby, rby) for n in (2, 3, 0, 1)]
+    ay[0].wait_recv()
+    ay[1].wait_recv()
+    ay += relay(lambda yy: A(yy, x), A_half, say, ray)
     ay[2].wait_recv()
+    ax += send_ax(1, y - 1)
     ay[3].wait_recv()
-    ay += relay(lambda yy: A(yy, x), A_half, say, ray)
-    ay[0].wait_recv()
-    ax += send_ax(1, y - 1)
-    ay[1].wait_recv()
     ax += send_ax(2, y + 1)
     ax += send_ax(3, y - 2)
     ax += send_ax(4, y + 2)
-    by[2].wait_recv()
-    by[3].wait_recv()
+    by[0].wait_recv()
+    by[1].wait_recv()
     by += relay(BY, B_half, sby, rby)
+    ay[6].wait_recv()
+    ax += send_ax(5, y - 3)
+    ay[7].wait_recv()
+    ax += send_ax(6, y + 3)
     ay[4].wait_recv()
-    ax += send_ax(5, y - 3)
     ay[5].wait_recv()
-    ax += send_ax(6, y + 3)
-    ay[6].wait_recv()
-    ay[7].wait_recv()
     ax += send_ax(7, y + 4)
-    for c in by[:2] + by[4:] + ax:
+    for c in by[2:] + ax:
         c.wait_recv()
 
     top = lax.broadcasted_iota(jnp.int32, (8, BINS), 0) < 4
 
-    def slots(ks):
+    def products(zt):
         tiles = []
-        for k in ks:
-            blk = plan[0, k]
+        for n in range(3):
+            blk = plan[0, 2 * zt + n]
             tiles.append((blk // NX, blk % NX))
-        acc = [[[None, None] for _ in range(4)] for _ in ks]
+        acc = [[[None, None] for _ in range(4)] for _ in tiles]
         for h in range(NT):
-            g = [G[by, bx_, tile(h)].astype(f32) for by, bx_ in tiles]
+            g = [G[py, px, tile(h)].astype(f32) for py, px in tiles]
             for a in range(4):
                 for c in range(2):
                     o = own[h, 4 * c + a]
-                    for n in range(len(ks)):
+                    for n in range(3):
                         p = o * g[n]
                         acc[n][a][c] = p if h == 0 else acc[n][a][c] + p
-        for n, k in enumerate(ks):
+        for n in range(3):
             for a in range(4):
                 p, q = acc[n][a]
                 re = p + pltpu.roll(q, 4, 0)
                 im = q - pltpu.roll(p, 4, 0)
-                stack[4 * k + a, :, 0:BINS] = re[0:4].astype(bf16)
-                stack[4 * k + a, :, BINS:2 * BINS] = im[0:4].astype(bf16)
-            by, bx_ = tiles[n]
-            fl = G[by, bx_, CUT].astype(f32)
-            of = G[y, x, CUT].astype(f32)
-            fe = jnp.where(top, fl, pltpu.roll(fl, 4, 0))
-            for half in range(2):
-                oa = jnp.where(top, jnp.broadcast_to(of[2 * half:2 * half + 1], (8, BINS)),
-                               jnp.broadcast_to(of[2 * half + 1:2 * half + 2], (8, BINS)))
-                pairs[2 * k + half] = fe * oa
-
-    slots([0])
-
-    def two(i, carry):
-        slots([2 * i + 1, 2 * i + 2])
+                stack[zt, 4 * n + a, :, 0:BINS] = re[0:4].astype(bf16)
+                stack[zt, 4 * n + a, :, BINS:2 * BINS] = im[0:4].astype(bf16)
+        return tiles
+
+    def offset(zt, c):
+        return 2 * zt + ROWS * c
+
+    def rows_to(i, dz, dc):
+        zt, c = (z + dz) % 8, (core + dc) % 2
+        return pltpu.make_async_remote_copy(
+            src_ref=stack.at[zt, pl.ds(offset(zt, c) // 4, 5)], dst_ref=recv.at[2 * i + dc],
+            send_sem=s4.at[2 * i + dc], recv_sem=r4.at[2 * i + dc],
+            device_id={"tm": 2 * zt + c}, device_id_type=pl.DeviceIdType.MESH)
+
+    def give(i, carry):
+        dz = 4 + (i + 1) // 2 * (2 * (i % 2) - 1)
+        products((z + dz) % 8)
+        for dc in (0, 1):
+            rows_to(i, dz, dc).start()
         return carry
 
-    lax.fori_loop(0, 8, two, 0)
-
-    last = {}
-    for dz, dc in reversed(PEERS):
-        to = line(dz, dc)
-        c = pltpu.make_async_remote_copy(
-            src_ref=stack.at[pl.ds(ROWS * to // 4, 5)], dst_ref=recv.at[slot(-dz, dc)],
-            send_sem=s4.at[slot(-dz, dc)], recv_sem=r4.at[slot(-dz, dc)],
-            device_id={"tm": to}, device_id_type=pl.DeviceIdType.MESH)
-        c.start()
-        last[slot(-dz, dc)] = c
+    lax.fori_loop(0, 7, give, 0)
+    tiles = products(z)
+    rows_to(7, 0, 1).start()
+
+    of = G[y, x, CUT].astype(f32)
+    for n, (py, px) in enumerate(tiles):
+        fl = G[py, px, CUT].astype(f32)
+        fe = jnp.where(top, fl, pltpu.roll(fl, 4, 0))
+        for half in range(2):
+            oa = jnp.where(top, jnp.broadcast_to(of[2 * half:2 * half + 1], (8, BINS)),
+                           jnp.broadcast_to(of[2 * half + 1:2 * half + 2], (8, BINS)))
+            pairs[2 * n + half] = fe * oa
+
     def rows(read):
         pad = jnp.zeros((4, 2 * BINS), f32)
         return jnp.concatenate([read(i).astype(f32) for i in range(5)] + [pad], axis=0).astype(bf16)
@@ -246,20 +253,22 @@
     def align(v, shift):
         return pltpu.roll(v, (24 - shift) % 24, 0)[0:ROWS]
 
-    first_row = ROWS * t // 8
-    counts = jnp.concatenate([pairs[first_row + i] for i in range(3)], axis=0)
-    counts = align(jnp.broadcast_to(jnp.sum(counts, axis=1, keepdims=True), (24, BINS)), ROWS * t % 8)
+    start = offset(z, core)
+    counts = jnp.concatenate([pairs[start // 8 + i] for i in range(3)], axis=0)
+    counts = align(jnp.broadcast_to(jnp.sum(counts, axis=1, keepdims=True), (24, BINS)), start % 8)
     gain = jnp.concatenate([(4.0 / math.sqrt(HALF)) / counts] * (LAGS // BINS), axis=1)
-    first_row = ROWS * t // 4
-    mine = rows(lambda i: stack[first_row + i])
+    mine = rows(lambda i: stack[z, start // 4 + i])
     acc = jnp.dot(mine, tab[t], preferred_element_type=f32)
-    for dz, dc in PEERS:
-        n = slot(dz, dc)
-        last[n].wait_recv()
-        lhs = rows(lambda i: recv[n, i])
-        acc = acc + jnp.dot(lhs, tab[line(dz, dc)], preferred_element_type=f32)
-    out_ref[...] = align(acc, ROWS * t % 4) * gain
-    for c in list(first.values()) + sends + list(last.values()):
+    last = []
+    for i, dz in reversed(list(enumerate(ORDER))):
+        for dc in ((0, 1) if dz else (1,)):
+            c = rows_to(i, dz, dc)
+            last.append(c)
+            c.wait_recv()
+            lhs = rows(lambda n: recv[2 * i + dc, n])
+            acc = acc + jnp.dot(lhs, tab[line(-dz, dc)], preferred_element_type=f32)
+    out_ref[...] = align(acc, start % 4) * gain
+    for c in list(first.values()) + sends + last:
         c.wait_send()
 
 
@@ -282,10 +291,10 @@
             pltpu.VMEM((NT, 16, BINS), bf16),
             pltpu.VMEM((NY, NX, TILES, 8, BINS), bf16),
             pltpu.VMEM((NT, 8, 8, BINS), f32),
-            pltpu.VMEM((4 * SLOTS, 4, 2 * BINS), bf16),
+            pltpu.VMEM((8, 12, 4, 2 * BINS), bf16),
             pltpu.VMEM((NT, 5, 4, 2 * BINS), bf16),
             pltpu.VMEM((NT, 2 * BINS, LAGS), bf16),
-            pltpu.VMEM((2 * SLOTS, 8, BINS), f32),
+            pltpu.VMEM((6, 8, BINS), f32),
             dma((5,)), dma((NT,)), dma((NT,)), dma((8,)), dma((8,)),
             dma((NY, NX)), dma((NY, NX)), dma((NX,)), dma((NX,)),
             dma((8,)), dma((8,)), dma((NT,)), dma((NT,)),

time: 42.3 us -> 41.3 us (0.976)
  Pallas kernels: 41.5 us -> 40.5 us
    pallas_call x1, Pallas kernels: 41.5 us -> 40.5 us  [per_device(): pl.pallas_call(kernel, out_shape=jax.ShapeDtypeStruct((ROWS, LAGS), f32),...]
where the time goes in v4:
time: 41.3 us; the launch traced here: 41.1 us
  Pallas kernels  40.5 us (98%)
  local copies, waits for them, and re-layouts  0.62 us (2%)
    pallas_call x1, Pallas kernels, per_device(): pl.pallas_call(kernel, out_shape=jax.ShapeDtypeStruct((ROWS, LAGS), f32),...  40.5 us

profile of v4, /device:TPU:1, one launch (start us, length us, event | category | flops | bytes accessed | tf_op | source)
XLA Modules:
  0.0 41.1 jit_solution(14024929066268860718)
XLA Ops:
  0.0 40.5 %shard_map.55 = f32[17,512]{1,0:T(8,128)S(1)} custom-call(s32[1,17]{1,0:T(1,128)} %plan_ref.1, s32[1,4]{1,0:T(1,128)} %valid_ref.1, bf16[1,4,4096]{2,1,0:T(4,128)(2,1)} %spectra_ref.1, f32[2,128,512]{2,1,0:T(8,128)} %constant.4.clone.base_ref, f32[2,16,512]{2,1,0:T(8,128)} %constant.5.clone.turn_ref), custom_call_target="tpu_custom_call" | custom-call | tf_op jit(solution)/shard_map/pallas_call | solution.py:279
  40.5 0.6 %copy.7 = f32[17,512]{1,0:T(8,128)} copy(f32[17,512]{1,0:T(8,128)S(1)} %shard_map.55) | data formatting | bytes 69632

commit v5 on v4

--- a/solution.py
+++ b/solution.py
@@ -16,7 +16,7 @@
 HALF = 2048
 BINS = HALF // NT
 TILES = 17
-CUT = 13
+CUT = 11
 DIST = (0, 1, 7, 2, 6, 3, 5, 4)
 ORDER = (4, 5, 3, 6, 2, 7, 1, 0)
 PEERS = [(dz, dc) for dz in DIST for dc in (0, 1)][1:]
@@ -69,7 +69,7 @@
     for j in range(1, NX):
         pl.semaphore_signal(barrier, inc=1, device_id=plane(y, x + j),
                             device_id_type=pl.DeviceIdType.MESH)
-    for j in (1, 2, NY - 2, NY - 1):
+    for j in (1, 2, 3, 5, 6, 7):
         pl.semaphore_signal(barrier, inc=1, device_id=plane(y + j, x),
                             device_id_type=pl.DeviceIdType.MESH)
 
@@ -84,7 +84,7 @@
         im = x_ref[0, :, HALF + j * BINS:HALF + (j + 1) * BINS].astype(f32) * flag
         msg[j] = jnp.concatenate([re, im, flag, flag], axis=0).astype(bf16)
 
-    pl.semaphore_wait(barrier, NT - 1 + NX - 1 + 4)
+    pl.semaphore_wait(barrier, NT - 1 + NX - 1 + 6)
 
     first = {}
     for dz, dc in reversed(PEERS):
@@ -145,6 +145,17 @@
         n = TILES - CUT
         return G.at[yy % NY, :, pl.ds(CUT + h * (n // 2), n // 2 if h == 0 else n - n // 2)]
 
+    def direct(block, ssem, rsem):
+        return {j: send(block, plane(y + j, x), ssem.at[j], rsem.at[j]) for j in (3, 5, 2, 6, 1, 7)}
+
+    def fourth(half, ssem, rsem):
+        return [send(half(y - 3, 0), plane(y + 1, x), ssem.at[0], rsem.at[0]),
+                send(half(y + 3, 1), plane(y - 1, x), ssem.at[4], rsem.at[4])]
+
+    def land(cs):
+        for c in cs:
+            c.wait_recv()
+
     def arrive(n):
         if n > 0:
             first[n].wait_recv()
@@ -152,7 +163,7 @@
 
     for n in range(CUT):
         arrive(n)
-    ay = [far(A(y, x), n, say, ray) for n in (2, 3, 0, 1)]
+    ay = direct(A(y, x), say, ray)
     for n in range(CUT, NT):
         arrive(n)
     lane = lax.broadcasted_iota(jnp.int32, (8, BINS), 1)
@@ -161,7 +172,6 @@
         flags = jnp.where(lane == n, got[n, 8:16].astype(f32), flags)
     G[y, x, CUT] = flags.astype(bf16)
     bx = [send(B(y, x), plane(y, x + j), sbx.at[j], rbx.at[j]) for j in range(1, NX)]
-    ax = send_ax(0, y)
     for n in range(NT):
         mine = got[n, 0:8].astype(f32)
         for q in range(8):
@@ -169,27 +179,21 @@
     for c in bx:
         c.wait_recv()
     by = [far(BY(y), n, sby, rby) for n in (2, 3, 0, 1)]
-    ay[0].wait_recv()
-    ay[1].wait_recv()
-    ay += relay(lambda yy: A(yy, x), A_half, say, ray)
-    ay[2].wait_recv()
-    ax += send_ax(1, y - 1)
-    ay[3].wait_recv()
-    ax += send_ax(2, y + 1)
-    ax += send_ax(3, y - 2)
-    ax += send_ax(4, y + 2)
-    by[0].wait_recv()
-    by[1].wait_recv()
+    ax = send_ax(0, y)
+    for n, j in enumerate((1, 7)):
+        ay[j].wait_recv()
+        ax += send_ax(n + 1, y - j)
+    land([ay[3], ay[5]])
+    a4 = fourth(A_half, say, ray)
+    for n, j in enumerate((3, 5, 2, 6)):
+        if n >= 2:
+            ay[j].wait_recv()
+        ax += send_ax(n + 3, y - j)
+    land(by[:2])
     by += relay(BY, B_half, sby, rby)
-    ay[6].wait_recv()
-    ax += send_ax(5, y - 3)
-    ay[7].wait_recv()
-    ax += send_ax(6, y + 3)
-    ay[4].wait_recv()
-    ay[5].wait_recv()
+    land(a4)
     ax += send_ax(7, y + 4)
-    for c in by[2:] + ax:
-        c.wait_recv()
+    land(by[2:] + ax)
 
     top = lax.broadcasted_iota(jnp.int32, (8, BINS), 0) < 4
 
@@ -257,6 +261,8 @@
     counts = jnp.concatenate([pairs[start // 8 + i] for i in range(3)], axis=0)
     counts = align(jnp.broadcast_to(jnp.sum(counts, axis=1, keepdims=True), (24, BINS)), start % 8)
     gain = jnp.concatenate([(4.0 / math.sqrt(HALF)) / counts] * (LAGS // BINS), axis=1)
+    for c in list(first.values()) + sends:
+        c.wait_send()
     mine = rows(lambda i: stack[z, start // 4 + i])
     acc = jnp.dot(mine, tab[t], preferred_element_type=f32)
     last = []
@@ -268,7 +274,7 @@
             lhs = rows(lambda n: recv[2 * i + dc, n])
             acc = acc + jnp.dot(lhs, tab[line(-dz, dc)], preferred_element_type=f32)
     out_ref[...] = align(acc, start % 4) * gain
-    for c in list(first.values()) + sends + last:
+    for c in last:
         c.wait_send()
 
 

time: 41.3 us -> 41.1 us (level)
  no operation moved by 1% of the time
where the time goes in v5:
time: 41.1 us; the launch traced here: 40.9 us
  Pallas kernels  40.3 us (98%)
  local copies, waits for them, and re-layouts  0.62 us (2%)
    pallas_call x1, Pallas kernels, per_device(): pl.pallas_call(kernel, out_shape=jax.ShapeDtypeStruct((ROWS, LAGS), f32),...  40.3 us

profile of v5, /device:TPU:1, one launch (start us, length us, event | category | flops | bytes accessed | tf_op | source)
XLA Modules:
  0.0 40.9 jit_solution(3642325482121219587)
XLA Ops:
  0.0 40.3 %shard_map.55 = f32[17,512]{1,0:T(8,128)S(1)} custom-call(s32[1,17]{1,0:T(1,128)} %plan_ref.1, s32[1,4]{1,0:T(1,128)} %valid_ref.1, bf16[1,4,4096]{2,1,0:T(4,128)(2,1)} %spectra_ref.1, f32[2,128,512]{2,1,0:T(8,128)} %constant.4.clone.base_ref, f32[2,16,512]{2,1,0:T(8,128)} %constant.5.clone.turn_ref), custom_call_target="tpu_custom_call" | custom-call | tf_op jit(solution)/shard_map/pallas_call | solution.py:285
  40.3 0.6 %copy.7 = f32[17,512]{1,0:T(8,128)} copy(f32[17,512]{1,0:T(8,128)S(1)} %shard_map.55) | data formatting | bytes 69632

commit v6 on v5

--- a/solution.py
+++ b/solution.py
@@ -20,7 +20,6 @@
 DIST = (0, 1, 7, 2, 6, 3, 5, 4)
 ORDER = (4, 5, 3, 6, 2, 7, 1, 0)
 PEERS = [(dz, dc) for dz in DIST for dc in (0, 1)][1:]
-HOP = (1, NY - 1, 2, NY - 2, 1, NY - 1, 2, NY - 2)
 f32, bf16 = jnp.float32, jnp.bfloat16
 
 
@@ -112,45 +111,36 @@
     lax.fori_loop(0, NT, fill, 0)
     sends = []
 
-    def send(ref, to, ssem, rsem):
-        c = pltpu.make_async_remote_copy(src_ref=ref, dst_ref=ref, send_sem=ssem, recv_sem=rsem,
+    def send(src, dst, to, ssem, rsem):
+        c = pltpu.make_async_remote_copy(src_ref=src, dst_ref=dst, send_sem=ssem, recv_sem=rsem,
                                          device_id=to, device_id_type=pl.DeviceIdType.MESH)
         c.start()
         sends.append(c)
         return c
 
-    def A(yy, xx):
-        return G.at[yy % NY, xx % NX, pl.ds(0, CUT)]
-
-    def B(yy, xx):
-        return G.at[yy % NY, xx % NX, pl.ds(CUT, TILES - CUT)]
-
-    def BY(yy):
-        return G.at[yy % NY, :, pl.ds(CUT, TILES - CUT)]
-
-    def send_ax(n, yy):
-        return [send(A(yy, x), plane(y, x + j), sax.at[n, j], rax.at[n, j]) for j in (2, 1, 3)]
-
-    def far(block, n, ssem, rsem):
-        return send(block, plane(y + HOP[n], x), ssem.at[n], rsem.at[n])
-
-    def relay(block, half, ssem, rsem):
-        return [far(half(y - 2, 0), 6, ssem, rsem), far(half(y + 2, 1), 7, ssem, rsem),
-                far(block(y - 2), 4, ssem, rsem), far(block(y + 2), 5, ssem, rsem)]
-
-    def A_half(yy, h):
-        return G.at[yy % NY, x, pl.ds(h * (CUT // 2), CUT // 2 if h == 0 else CUT - CUT // 2)]
-
-    def B_half(yy, h):
-        n = TILES - CUT
-        return G.at[yy % NY, :, pl.ds(CUT + h * (n // 2), n // 2 if h == 0 else n - n // 2)]
-
-    def direct(block, ssem, rsem):
-        return {j: send(block, plane(y + j, x), ssem.at[j], rsem.at[j]) for j in (3, 5, 2, 6, 1, 7)}
-
-    def fourth(half, ssem, rsem):
-        return [send(half(y - 3, 0), plane(y + 1, x), ssem.at[0], rsem.at[0]),
-                send(half(y + 3, 1), plane(y - 1, x), ssem.at[4], rsem.at[4])]
+    def place(o):
+        r = o % NY
+        return 2 * r if r < 4 else 15 - 2 * r
+
+    def cut_of(part, half):
+        lo, hi = part
+        mid = (lo + hi) // 2
+        return ((lo, hi), (lo, mid), (mid, hi))[half]
+
+    def A(o, half=0):
+        lo, hi = cut_of((0, CUT), half)
+        return G.at[place(o), x, pl.ds(lo, hi - lo)]
+
+    def BY(o, half=0):
+        lo, hi = cut_of((CUT, TILES), half)
+        return G.at[place(o), :, pl.ds(lo, hi - lo)]
+
+    def to_x(p, n, part, sems):
+        ref = G.at[pl.ds(p, n), x, pl.ds(part[0], part[1] - part[0])]
+        return [send(ref, ref, plane(y, x + j), sems[0].at[p, j], sems[1].at[p, j]) for j in (2, 1, 3)]
+
+    def to_y(block, o, j, n, sems, half=0):
+        return send(block(o, half), block(o - j, half), plane(y + j, x), sems[0].at[n], sems[1].at[n])
 
     def land(cs):
         for c in cs:
@@ -159,40 +149,41 @@
     def arrive(n):
         if n > 0:
             first[n].wait_recv()
-        G[y, x, tile(n)] = got[n, 0:8]
+        G[0, x, tile(n)] = got[n, 0:8]
 
     for n in range(CUT):
         arrive(n)
-    ay = direct(A(y, x), say, ray)
+    ay = {j: to_y(A, 0, j, j % NY, (say, ray)) for j in (3, -3, 2, -2, 1, -1)}
     for n in range(CUT, NT):
         arrive(n)
     lane = lax.broadcasted_iota(jnp.int32, (8, BINS), 1)
     flags = jnp.zeros((8, BINS), f32)
     for n in range(NT):
         flags = jnp.where(lane == n, got[n, 8:16].astype(f32), flags)
-    G[y, x, CUT] = flags.astype(bf16)
-    bx = [send(B(y, x), plane(y, x + j), sbx.at[j], rbx.at[j]) for j in range(1, NX)]
+    G[0, x, CUT] = flags.astype(bf16)
+    bx = to_x(0, 1, (CUT, TILES), (sbx, rbx))
     for n in range(NT):
         mine = got[n, 0:8].astype(f32)
         for q in range(8):
             own[n, q] = jnp.broadcast_to(mine[q:q + 1], (8, BINS))
     for c in bx:
         c.wait_recv()
-    by = [far(BY(y), n, sby, rby) for n in (2, 3, 0, 1)]
-    ax = send_ax(0, y)
-    for n, j in enumerate((1, 7)):
-        ay[j].wait_recv()
-        ax += send_ax(n + 1, y - j)
-    land([ay[3], ay[5]])
-    a4 = fourth(A_half, say, ray)
-    for n, j in enumerate((3, 5, 2, 6)):
-        if n >= 2:
-            ay[j].wait_recv()
-        ax += send_ax(n + 3, y - j)
+    yb = (sby, rby)
+    by = [to_y(BY, 0, j, n, yb) for n, j in enumerate((2, -2, 1, -1))]
+    xa = ((0, CUT), (sax, rax))
+    ax = to_x(0, 1, *xa)
+    land([ay[1], ay[-1]])
+    ax += to_x(1, 2, *xa)
+    land([ay[3], ay[-3]])
+    a4 = [to_y(A, -3, 1, 0, (say, ray), 1), to_y(A, 3, -1, 4, (say, ray), 2)]
+    land([ay[2], ay[-2]])
+    ax += to_x(3, 2, *xa)
+    ax += to_x(5, 2, *xa)
     land(by[:2])
-    by += relay(BY, B_half, sby, rby)
+    by += [to_y(BY, -2, 2, 4, yb, 1), to_y(BY, 2, -2, 5, yb, 2),
+           to_y(BY, -2, 1, 6, yb), to_y(BY, 2, -1, 7, yb)]
     land(a4)
-    ax += send_ax(7, y + 4)
+    ax += to_x(7, 1, *xa)
     land(by[2:] + ax)
 
     top = lax.broadcasted_iota(jnp.int32, (8, BINS), 0) < 4
@@ -201,7 +192,8 @@
         tiles = []
         for n in range(3):
             blk = plan[0, 2 * zt + n]
-            tiles.append((blk // NX, blk % NX))
+            r = (blk // NX + NY - y) % NY
+            tiles.append((jnp.where(r < 4, 2 * r, 15 - 2 * r), blk % NX))
         acc = [[[None, None] for _ in range(4)] for _ in tiles]
         for h in range(NT):
             g = [G[py, px, tile(h)].astype(f32) for py, px in tiles]
@@ -241,7 +233,7 @@
     tiles = products(z)
     rows_to(7, 0, 1).start()
 
-    of = G[y, x, CUT].astype(f32)
+    of = G[0, x, CUT].astype(f32)
     for n, (py, px) in enumerate(tiles):
         fl = G[py, px, CUT].astype(f32)
         fe = jnp.where(top, fl, pltpu.roll(fl, 4, 0))
@@ -302,7 +294,7 @@
             pltpu.VMEM((NT, 2 * BINS, LAGS), bf16),
             pltpu.VMEM((6, 8, BINS), f32),
             dma((5,)), dma((NT,)), dma((NT,)), dma((8,)), dma((8,)),
-            dma((NY, NX)), dma((NY, NX)), dma((NX,)), dma((NX,)),
+            dma((NY, NX)), dma((NY, NX)), dma((1, NX)), dma((1, NX)),
             dma((8,)), dma((8,)), dma((NT,)), dma((NT,)),
         ],
         compiler_params=pltpu.CompilerParams(

time: 41.1 us -> 41 us (level)
  no operation moved by 1% of the time
where the time goes in v6:
time: 41 us; the launch traced here: 40.9 us
  Pallas kernels  40.2 us (98%)
  local copies, waits for them, and re-layouts  0.62 us (2%)
    pallas_call x1, Pallas kernels, per_device(): pl.pallas_call(kernel, out_shape=jax.ShapeDtypeStruct((ROWS, LAGS), f32),...  40.2 us

profile of v6, /device:TPU:1, one launch (start us, length us, event | category | flops | bytes accessed | tf_op | source)
XLA Modules:
  0.0 40.9 jit_solution(9935381423722044650)
XLA Ops:
  0.0 40.2 %shard_map.55 = f32[17,512]{1,0:T(8,128)S(1)} custom-call(s32[1,17]{1,0:T(1,128)} %plan_ref.1, s32[1,4]{1,0:T(1,128)} %valid_ref.1, bf16[1,4,4096]{2,1,0:T(4,128)(2,1)} %spectra_ref.1, f32[2,128,512]{2,1,0:T(8,128)} %constant.4.clone.base_ref, f32[2,16,512]{2,1,0:T(8,128)} %constant.5.clone.turn_ref), custom_call_target="tpu_custom_call" | custom-call | tf_op jit(solution)/shard_map/pallas_call | solution.py:277
  40.3 0.6 %copy.7 = f32[17,512]{1,0:T(8,128)} copy(f32[17,512]{1,0:T(8,128)S(1)} %shard_map.55) | data formatting | bytes 69632

commit v7 on v4

--- a/solution.py
+++ b/solution.py
@@ -161,7 +161,6 @@
         flags = jnp.where(lane == n, got[n, 8:16].astype(f32), flags)
     G[y, x, CUT] = flags.astype(bf16)
     bx = [send(B(y, x), plane(y, x + j), sbx.at[j], rbx.at[j]) for j in range(1, NX)]
-    ax = send_ax(0, y)
     for n in range(NT):
         mine = got[n, 0:8].astype(f32)
         for q in range(8):
@@ -169,6 +168,7 @@
     for c in bx:
         c.wait_recv()
     by = [far(BY(y), n, sby, rby) for n in (2, 3, 0, 1)]
+    ax = send_ax(0, y)
     ay[0].wait_recv()
     ay[1].wait_recv()
     ay += relay(lambda yy: A(yy, x), A_half, say, ray)
@@ -257,6 +257,8 @@
     counts = jnp.concatenate([pairs[start // 8 + i] for i in range(3)], axis=0)
     counts = align(jnp.broadcast_to(jnp.sum(counts, axis=1, keepdims=True), (24, BINS)), start % 8)
     gain = jnp.concatenate([(4.0 / math.sqrt(HALF)) / counts] * (LAGS // BINS), axis=1)
+    for c in list(first.values()) + sends:
+        c.wait_send()
     mine = rows(lambda i: stack[z, start // 4 + i])
     acc = jnp.dot(mine, tab[t], preferred_element_type=f32)
     last = []
@@ -268,7 +270,7 @@
             lhs = rows(lambda n: recv[2 * i + dc, n])
             acc = acc + jnp.dot(lhs, tab[line(-dz, dc)], preferred_element_type=f32)
     out_ref[...] = align(acc, start % 4) * gain
-    for c in list(first.values()) + sends + last:
+    for c in last:
         c.wait_send()
 
 

time: 41.3 us -> 41.1 us (level)
  no operation moved by 1% of the time
where the time goes in v7:
time: 41.1 us; the launch traced here: 41 us
  Pallas kernels  40.3 us (98%)
  local copies, waits for them, and re-layouts  0.62 us (2%)
    pallas_call x1, Pallas kernels, per_device(): pl.pallas_call(kernel, out_shape=jax.ShapeDtypeStruct((ROWS, LAGS), f32),...  40.3 us

profile of v7, /device:TPU:1, one launch (start us, length us, event | category | flops | bytes accessed | tf_op | source)
XLA Modules:
  0.0 41.0 jit_solution(17098434042623556145)
XLA Ops:
  0.0 40.3 %shard_map.55 = f32[17,512]{1,0:T(8,128)S(1)} custom-call(s32[1,17]{1,0:T(1,128)} %plan_ref.1, s32[1,4]{1,0:T(1,128)} %valid_ref.1, bf16[1,4,4096]{2,1,0:T(4,128)(2,1)} %spectra_ref.1, f32[2,128,512]{2,1,0:T(8,128)} %constant.4.clone.base_ref, f32[2,16,512]{2,1,0:T(8,128)} %constant.5.clone.turn_ref), custom_call_target="tpu_custom_call" | custom-call | tf_op jit(solution)/shard_map/pallas_call | solution.py:281
  40.4 0.6 %copy.7 = f32[17,512]{1,0:T(8,128)} copy(f32[17,512]{1,0:T(8,128)S(1)} %shard_map.55) | data formatting | bytes 69632
